TPU v7x, 32 devices: a whole 2x2x4 slice. The times are simulated.
32 devices in a mesh: orow: 8 (over z, x), ocol: 4 (over y, core).
Axes of the slice: x: 2, y: 2, z: 4, core: 2. Of those that a mesh axis runs over, the one named last changes fastest.
Arguments:
- integrals: bfloat16 [2304, 16, 384], P('ocol', 'orow'), may hold values from -0.29882812 to 0.29882812
- occ_count: int32 [8], replicated, may hold values from 1 to 2
- occ_energy: float32 [16], replicated, may hold values from -2 to -0.5
- vir_energy: float32 [384], replicated, may hold values from 0.3 to 2.5
- task_iblock: int32 [32, 1], replicated, may hold values from 0 to 7; in each aligned block of 32 rows (0 to 31, 32 to 63, ...) at most 8 rows name the same one
- task_jblock: int32 [32], replicated, may hold values from 0 to 7
Outputs:
- gamma_out: float32 [2304, 16, 384], P('ocol', 'orow')
- density: float32 [384, 384], replicated
Inputs may be any that keep to these rules, and one draw needn't show every extreme that they name: `task_iblock`: no first block is named by more than 8 tasks, and some first block by exactly 8.
All inputs are finite; a program needn't handle non-finite values.
Results may differ from a plain program's by a relative error of at most 0.0019.
Values may be sent and summed in bfloat16 or wider, within the bound.
A program may use at most 128 MiB of HBM per device.

v0:
```python
import jax
import jax.numpy as jnp
from jax import lax
from jax.sharding import PartitionSpec as P


def make_amplitudes(k_total, i_energy, j_energy, vir_energy, usable):
    slots = k_total.shape[0]
    orbitals = i_energy.shape[1]
    virtuals = vir_energy.shape[0]
    k_grid = k_total.reshape(slots, orbitals, virtuals, orbitals, virtuals)
    denominator = (
        i_energy[:, :, None, None, None]
        + j_energy[:, None, None, :, None]
        - vir_energy[None, None, :, None, None]
        - vir_energy[None, None, None, None, :]
    )
    values = (2.0 * k_grid - jnp.swapaxes(k_grid, 2, 4)) / denominator
    values = values * usable[:, None, None, None, None]
    return values.astype(jnp.bfloat16).reshape(slots, orbitals * virtuals, orbitals * virtuals)


def local(integrals, occ_count, occ_energy, vir_energy, task_iblock, task_jblock):
    aux_local = integrals.shape[0]
    orbitals = integrals.shape[1]
    virtuals = integrals.shape[2]
    span = orbitals * virtuals
    block_total = lax.axis_size("orow")
    col_total = lax.axis_size("ocol")
    my_row = lax.axis_index("orow")
    my_col = lax.axis_index("ocol")
    active = jnp.arange(orbitals) < occ_count[my_row]
    masked = integrals * active.astype(jnp.bfloat16)[None, :, None]
    gathered = lax.all_gather(masked, "orow", axis=1, tiled=True)
    flat_blocks = gathered.reshape(aux_local, block_total, span)
    first_list = task_iblock[:, 0]
    task_total = first_list.shape[0]
    per_row = task_total // block_total
    task_ids = my_row * per_row + jnp.arange(per_row)
    i_block = first_list[task_ids]
    j_block = task_jblock[task_ids]
    usable = jnp.ones((per_row,), jnp.float32)
    energy_grid = occ_energy.reshape(block_total, orbitals)
    i_rows = jnp.take(flat_blocks, i_block, axis=1)
    j_rows = jnp.take(flat_blocks, j_block, axis=1)
    k_partial = jnp.einsum("psx,psy->sxy", i_rows, j_rows, preferred_element_type=jnp.float32)
    slots = k_partial.shape[0]
    i_energy = energy_grid[i_block]
    j_energy = energy_grid[j_block]
    k_total = lax.psum(k_partial, "ocol")
    amplitudes = make_amplitudes(k_total, i_energy, j_energy, vir_energy, usable)
    gamma_i = jnp.einsum("sxy,psy->psx", amplitudes, j_rows, preferred_element_type=jnp.float32)
    gamma_j = jnp.einsum("sxy,psx->psy", amplitudes, i_rows, preferred_element_type=jnp.float32)
    slice_width = span // col_total
    amp_grid = amplitudes.reshape(slots, orbitals, virtuals, span)
    column_part = lax.dynamic_slice_in_dim(amp_grid, my_col * slice_width, slice_width, 3)
    dens_part = jnp.einsum(
        "siaw,sibw->ab", column_part, column_part, preferred_element_type=jnp.float32
    )
    block_ids = jnp.arange(block_total)
    i_onehot = (i_block[:, None] == block_ids[None, :]).astype(jnp.float32)
    j_onehot = (j_block[:, None] == block_ids[None, :]).astype(jnp.float32)
    buffer = jnp.einsum(
        "sk,psx->pkx", i_onehot, gamma_i, precision=lax.Precision.HIGHEST
    ) + jnp.einsum("sk,psx->pkx", j_onehot, gamma_j, precision=lax.Precision.HIGHEST)
    owned = lax.psum_scatter(buffer, "orow", scatter_dimension=1, tiled=True)
    gamma_out = owned.reshape(aux_local, orbitals, virtuals)
    density = lax.psum(dens_part, ("orow", "ocol")) / task_total
    return (gamma_out, density)


def solution(mesh):
    return jax.shard_map(
        local,
        mesh=mesh,
        in_specs=(P("ocol", "orow", None), P(), P(), P(), P(), P()),
        out_specs=(P("ocol", "orow", None), P()),
        check_vma=False,
    )
```

profile of v0, /device:TPU:0, one launch (start us, length us, event | category | flops | bytes accessed | tf_op | source)
XLA Modules:
  0.0 801.5 jit_solution(11271543090973514411)
XLA Ops:
  7.2 1.2 dynamic_slice.6
  8.5 0.6 compare_convert_fusion
  9.1 2.3 copy_multiply_fusion
  11.5 0.6 gather_fusion.1
  12.1 1.3 gather_fusion
  14.0 108.6 %all-gather.2.cloned.1.call-done = bf16[576,16,384]{2,0,1:T(8,128)(2,1)} async-done(((bf16[576,2,384]{2,0,1:T(8,128)(2,1)}), bf16[576,16,384]{2,0,1:T(8,128)(2,1)}) %all-gather.2.cloned.1.call-update) | async-done | bytes 7077904 | tf_op jit(solution)/shard_map/all_gather | solution.py:34
  122.6 10.1 %copy.40 = bf16[576,16,384]{2,1,0:T(8,128)(2,1)} copy(bf16[576,16,384]{2,0,1:T(8,128)(2,1)} %all-gather.2.cloned.1.call-done) | data formatting | bytes 14155776 | tf_op jit(solution)/shard_map/all_gather | solution.py:34
  132.7 11.3 %reshape.89 = bf16[576,8,768]{2,1,0:T(8,128)(2,1)} reshape(bf16[576,16,384]{2,1,0:T(8,128)(2,1)} %copy.40) | data formatting | bytes 14155776 | tf_op jit(solution)/shard_map/reshape | solution.py:35
  144.0 7.4 copy.41
  151.4 5.6 gather_fusion.5
  157.0 3.8 gather_fusion.4
  160.8 9.3 %fusion.7 = f32[4,768,768]{2,1,0:T(8,128)} fusion(bf16[4,576,768]{2,1,0:T(8,128)(2,1)S(1)} %gather_fusion.4, pred[4]{0:T(512)(128)(4,1)S(1)} %get-tuple-element.4, bf16[4,576,768]{2,1,0:T(8,128)(2,1)} %gather_fusion.5, pred[4]{0:T(512)(128)(4,1)S(1)} %copy-done.11), kind=kOutput, calls=%fused_computation.15 | convolution fusion | flops 2721447936 | bytes 16515080 | tf_op jit(solution)/shard_map/psx,psy->sxy/dot_general | solution.py:46
  170.1 12.5 %reshape.90 = f32[4,2,384,2,384]{4,3,2,1,0:T(2,128)} reshape(f32[4,768,768]{2,1,0:T(8,128)} %fusion.7) | data formatting | bytes 18874368 | tf_op jit(solution)/shard_map/reshape | solution.py:11
  182.6 14.8 %copy.43 = f32[4,2,384,2,384]{2,4,3,1,0:T(8,128)} copy(f32[4,2,384,2,384]{4,3,2,1,0:T(2,128)} %reshape.90) | data formatting | bytes 18874368 | tf_op jit(solution)/shard_map/reshape | solution.py:11
  199.9 0.7 gather_fusion.2
  200.7 0.7 broadcast_subtract_fusion
  201.4 164.2 %all-reduce.3.cloned.1.call-done = f32[4,2,384,2,384]{2,4,3,1,0:T(8,128)} async-done(((f32[4,2,384,2,384]{2,4,3,1,0:T(8,128)}), f32[4,2,384,2,384]{2,4,3,1,0:T(8,128)}) %all-reduce.3.cloned.1.call-update) | async-done | bytes 9437200 | tf_op jit(solution)/shard_map/psum | solution.py:50
  365.6 9.6 %copy.44 = f32[4,2,384,2,384]{4,2,3,1,0:T(8,128)} copy(f32[4,2,384,2,384]{2,4,3,1,0:T(8,128)} %all-reduce.3.cloned.1.call-done) | data formatting | bytes 18874368 | tf_op jit(solution)/shard_map/psum | solution.py:50
  375.2 9.6 %fusion.1 = bf16[4,2,384,2,384]{4,2,3,1,0:T(8,128)(2,1)} fusion(f32[4,2,384,2,384]{2,4,3,1,0:T(8,128)} %all-reduce.3.cloned.1.call-done, f32[4,2,384,2,384]{4,2,3,1,0:T(8,128)} %copy.44, f32[384]{0:T(512)S(1)} %copy-done.3, f32[4,2,384,2]{2,3,1,0:T(2,128)} %broadcast_subtract_fusion), kind=kLoop, calls=%fused_computation.9 | loop fusion | flops 11796480 | bytes 23619072 | tf_op jit(solution)/shard_map/convert_element_type | solution.py:20
  384.8 6.7 copy.52
  391.5 9.3 %copy.45 = bf16[4,2,384,2,384]{4,3,2,1,0:T(2,128)(2,1)} copy(bf16[4,2,384,2,384]{4,2,3,1,0:T(8,128)(2,1)} %fusion.1) | data formatting | bytes 9437184 | tf_op jit(solution)/shard_map/convert_element_type | solution.py:20
  400.8 11.3 %reshape.92 = bf16[4,768,768]{2,1,0:T(8,128)(2,1)} reshape(bf16[4,2,384,2,384]{4,3,2,1,0:T(2,128)(2,1)} %copy.45) | data formatting | bytes 9437184 | tf_op jit(solution)/shard_map/reshape | solution.py:20
  412.1 9.4 %fusion.15 = f32[576,4,768]{2,0,1:T(8,128)} fusion(bf16[4,768,768]{2,1,0:T(8,128)(2,1)} %reshape.92, bf16[4,576,768]{2,1,0:T(8,128)(2,1)} %gather_fusion.5, pred[4]{0:T(512)(128)(4,1)S(1)} %copy-done.12), kind=kOutput, calls=%fused_computation.23 | convolution fusion | flops 2719678464 | bytes 15335428 | tf_op jit(solution)/shard_map/sxy,psx->psy/dot_general | solution.py:53
  421.5 5.2 fusion.12
  426.8 3.3 convolution_bitcast_fusion
  430.1 14.4 %fusion.3 = f32[576,768,8]{1,2,0:T(8,128)S(1)} fusion(f32[576,4,768]{2,0,1:T(8,128)} %fusion.12, s32[4]{0:T(128)S(1)} %copy-done.5), kind=kOutput, calls=%fused_computation.11 | convolution fusion | flops 169869344 | bytes 21233680 | tf_op jit(solution)/shard_map/sk,psx->pkx/dot_general | solution.py:63
  444.6 18.4 %add_bitcast_fusion = f32[576,8,768]{2,1,0:T(8,128)} fusion(f32[576,768,8]{1,2,0:T(8,128)S(1)} %fusion.3, f32[576,4,768]{2,0,1:T(8,128)} %fusion.15, s32[4]{0:T(128)S(1)} %copy-done.7), kind=kOutput, calls=%fused_computation.6 | convolution fusion | flops 173408288 | bytes 35389456 | tf_op jit(solution)/shard_map/sk,psx->pkx/dot_general | solution.py:65
  462.9 14.7 %copy.48 = f32[576,8,768]{2,0,1:T(8,128)} copy(f32[576,8,768]{2,1,0:T(8,128)} %add_bitcast_fusion) | data formatting | bytes 28311552 | tf_op jit(solution)/shard_map/add | solution.py:63
  477.6 80.9 %all-reduce.5.cloned.1.call-done = f32[384,384]{1,0:T(8,128)} async-done(((f32[384,384]{1,0:T(8,128)}), f32[384,384]{1,0:T(8,128)}) %all-reduce.5.cloned.1.call-update) | async-done | bytes 589840 | tf_op jit(solution)/shard_map/psum | solution.py:68
  558.5 1.9 broadcast_multiply_fusion
  560.5 231.3 %reduce-scatter.2.cloned.1.call-done = f32[576,1,768]{2,0,1:T(8,128)} async-done(((f32[576,8,768]{2,0,1:T(8,128)}), f32[576,1,768]{2,0,1:T(8,128)}) %reduce-scatter.2.cloned.1.call-update) | async-done | bytes 1769488 | tf_op jit(solution)/shard_map/reduce_scatter | solution.py:66
  791.7 3.1 reshape.93
  (48 shorter events, 3.3 us)
Async XLA Ops:
  7.2 4.3 copy-start
  7.2 115.4 %all-gather.2.cloned.1.call-start = ((), (), s32[]{:S(2)}) async-start(), calls=%async_computation.1 | async-start | bytes 7962624 | tf_op jit(solution)/shard_map/all_gather | solution.py:34
  11.4 354.2 %all-reduce.3.cloned.1.call-start = ((), (), s32[]{:S(2)}) async-start(), calls=%async_computation.2 | async-start | bytes 18874368 | tf_op jit(solution)/shard_map/psum | solution.py:50
  12.1 120.6 %copy-start.4 = (s32[4]{0:T(128)}, s32[4]{0:T(128)S(1)}, u32[]{:S(2)}) copy-start(s32[4]{0:T(128)S(1)} %gather_fusion.1) | copy-start | bytes 52
  13.4 184.7 %copy-start.6 = (s32[4]{0:T(128)}, s32[4]{0:T(128)S(1)}, u32[]{:S(2)}) copy-start(s32[4]{0:T(128)S(1)} %gather_fusion) | copy-start | bytes 52
  14.0 146.8 %copy-start.9 = (pred[4]{0:T(512)(128)(4,1)}, pred[4]{0:T(512)(128)(4,1)S(1)}, u32[]{:S(2)}) copy-start(pred[4]{0:T(512)(128)(4,1)S(1)} %get-tuple-element.4) | copy-start | bytes 16
  157.0 3.8 copy-start.11
  197.4 0.7 copy-start.8
  197.4 3.3 copy-start.3
  197.4 361.1 %all-reduce.5.cloned.1.call-start = ((), (), s32[]{:S(2)}) async-start(), calls=%async_computation.4 | async-start | bytes 1179648 | tf_op jit(solution)/shard_map/psum | solution.py:68
  400.8 11.4 %copy-start.12 = (pred[4]{0:T(512)(128)(4,1)S(1)}, pred[4]{0:T(512)(128)(4,1)}, u32[]{:S(2)}) copy-start(pred[4]{0:T(512)(128)(4,1)} %get-tuple-element.3) | copy-start | bytes 16
  412.1 9.4 %copy-start.2 = (bf16[4,768,768]{2,1,0:T(8,128)(2,1)S(1)}, bf16[4,768,768]{2,1,0:T(8,128)(2,1)}, u32[]{:S(2)}) copy-start(bf16[4,768,768]{2,1,0:T(8,128)(2,1)} %reshape.92) | copy-start | bytes 14155780
  412.1 9.4 %copy-start.10 = (pred[4]{0:T(512)(128)(4,1)S(1)}, pred[4]{0:T(512)(128)(4,1)}, u32[]{:S(2)}) copy-start(pred[4]{0:T(512)(128)(4,1)} %copy-done.9) | copy-start | bytes 16
  421.5 8.6 %copy-start.5 = (s32[4]{0:T(128)S(1)}, s32[4]{0:T(128)}, u32[]{:S(2)}) copy-start(s32[4]{0:T(128)} %copy-done.4) | copy-start | bytes 52
  430.1 14.5 %copy-start.7 = (s32[4]{0:T(128)S(1)}, s32[4]{0:T(128)}, u32[]{:S(2)}) copy-start(s32[4]{0:T(128)} %copy-done.6) | copy-start | bytes 52
  430.1 361.6 %reduce-scatter.2.cloned.1.call-start = ((), (), s32[]{:S(2)}) async-start(), calls=%async_computation.3 | async-start | bytes 15925248 | tf_op jit(solution)/shard_map/reduce_scatter | solution.py:66
  477.6 317.1 %copy-start.1 = (s32[32,1]{0,1:T(1,128)S(1)}, s32[32,1]{0,1:T(1,128)}, u32[]{:S(2)}) copy-start(s32[32,1]{0,1:T(1,128)} %param.12) | copy-start | bytes 388
Sparse Core Ops, SparseCore 0:
  11.5 111.0 all-gather.1
  197.6 167.9 all-reduce.2
  430.2 128.3 all-reduce.4
  562.0 229.6 reduce-scatter.1
where the time goes:
time: 811 us; the launch traced here: 802 us
  waiting for transfers between devices  585 us (72%)
  local copies, waits for them, and re-layouts  125 us (15%)
  matrix products  60 us (7%)
  other arithmetic  16.9 us (2%)
  between operations  14.2 us (2%)
    reduce_scatter x1, waiting for transfers between devices, local(): owned = lax.psum_scatter(buffer, 'orow', scatter_dimension=1, tiled=True)  231 us
    psum x1, waiting for transfers between devices, local(): k_total = lax.psum(k_partial, 'ocol')  164 us
    all_gather x1, waiting for transfers between devices, local(): gathered = lax.all_gather(masked, 'orow', axis=1, tiled=True)  109 us
    psum x1, waiting for transfers between devices, local(): density = lax.psum(dens_part, ('orow', 'ocol')) / task_total  80.9 us
    reshape x2, local copies, waits for them, and re-layouts, make_amplitudes(): k_grid = k_total.reshape(slots, orbitals, virtuals, orbitals, virtuals)  27.3 us
    reshape x2, local copies, waits for them, and re-layouts, local(): flat_blocks = gathered.reshape(aux_local, block_total, span)  18.6 us
    dot_general x1, matrix products, local(): jnp.einsum('sk,psx->pkx', j_onehot, gamma_j, precision=lax.Precision.HIGH...  18.4 us
  transfers between devices with their start and end apart: 4, of which 4 were waited for; matrix products, arithmetic and copies ran while one was open for 7% of the time, Pallas kernels for 0%

commit v1 on v0

--- a/solution.py
+++ b/solution.py
@@ -65,7 +65,7 @@
     ) + jnp.einsum("sk,psx->pkx", j_onehot, gamma_j, precision=lax.Precision.HIGHEST)
     owned = lax.psum_scatter(buffer, "orow", scatter_dimension=1, tiled=True)
     gamma_out = owned.reshape(aux_local, orbitals, virtuals)
-    density = lax.psum(dens_part, ("orow", "ocol")) / task_total
+    density = lax.psum(lax.psum(dens_part, "ocol"), "orow") / task_total
     return (gamma_out, density)
 
 

time: 811 us -> 792 us (0.977)
  waiting for transfers between devices: 585 us -> 561 us
    psum x1 -> x2, waiting for transfers between devices: 80.9 us -> 58 us  [local(): density = lax.psum(lax.psum(dens_part, 'ocol'), 'orow') / task_total]
  transfers between devices with their start and end apart: 4 -> 5, of which waited for: 4 -> 5; matrix products, arithmetic and copies ran while one was open for 7% -> 8% of each run, Pallas kernels for 0% -> 0%
where the time goes in v1:
time: 792 us; the launch traced here: 782 us
  waiting for transfers between devices  561 us (71%)
  local copies, waits for them, and re-layouts  125 us (16%)
  matrix products  64.9 us (8%)
  other arithmetic  16.9 us (2%)
  between operations  14.2 us (2%)
    reduce_scatter x1, waiting for transfers between devices, local(): owned = lax.psum_scatter(buffer, 'orow', scatter_dimension=1, tiled=True)  230 us
    psum x1, waiting for transfers between devices, local(): k_total = lax.psum(k_partial, 'ocol')  164 us
    all_gather x1, waiting for transfers between devices, local(): gathered = lax.all_gather(masked, 'orow', axis=1, tiled=True)  109 us
    psum x2, waiting for transfers between devices, local(): density = lax.psum(lax.psum(dens_part, 'ocol'), 'orow') / task_total  58 us
    reshape x2, local copies, waits for them, and re-layouts, make_amplitudes(): k_grid = k_total.reshape(slots, orbitals, virtuals, orbitals, virtuals)  27.3 us
    dot_general x1, matrix products, local(): jnp.einsum('sk,psx->pkx', j_onehot, gamma_j, precision=lax.Precision.HIGH...  20.2 us
    reshape x2, local copies, waits for them, and re-layouts, local(): flat_blocks = gathered.reshape(aux_local, block_total, span)  18.6 us
    dot_general x1, matrix products, local(): jnp.einsum('sk,psx->pkx', i_onehot, gamma_i, precision=lax.Precision.HIGH...  17.5 us
  transfers between devices with their start and end apart: 5, of which 5 were waited for; matrix products, arithmetic and copies ran while one was open for 8% of the time, Pallas kernels for 0%

profile of v1, /device:TPU:0, one launch (start us, length us, event | category | flops | bytes accessed | tf_op | source)
XLA Modules:
  0.0 782.3 jit_solution(8443943927913695250)
XLA Ops:
  7.2 1.2 dynamic_slice.6
  8.5 0.6 compare_convert_fusion
  9.1 2.3 copy_multiply_fusion
  12.1 1.3 gather_fusion
  14.0 108.6 %all-gather.2.cloned.1.call-done = bf16[576,16,384]{2,0,1:T(8,128)(2,1)} async-done(((bf16[576,2,384]{2,0,1:T(8,128)(2,1)}), bf16[576,16,384]{2,0,1:T(8,128)(2,1)}) %all-gather.2.cloned.1.call-update) | async-done | bytes 7077904 | tf_op jit(solution)/shard_map/all_gather | solution.py:34
  122.6 10.1 %copy.40 = bf16[576,16,384]{2,1,0:T(8,128)(2,1)} copy(bf16[576,16,384]{2,0,1:T(8,128)(2,1)} %all-gather.2.cloned.1.call-done) | data formatting | bytes 14155776 | tf_op jit(solution)/shard_map/all_gather | solution.py:34
  132.7 11.3 %reshape.89 = bf16[576,8,768]{2,1,0:T(8,128)(2,1)} reshape(bf16[576,16,384]{2,1,0:T(8,128)(2,1)} %copy.40) | data formatting | bytes 14155776 | tf_op jit(solution)/shard_map/reshape | solution.py:35
  144.0 7.4 copy.41
  151.4 5.6 gather_fusion.5
  157.0 3.8 gather_fusion.4
  160.8 9.3 %fusion.7 = f32[4,768,768]{2,1,0:T(8,128)} fusion(bf16[4,576,768]{2,1,0:T(8,128)(2,1)S(1)} %gather_fusion.4, pred[4]{0:T(512)(128)(4,1)S(1)} %get-tuple-element.4, bf16[4,576,768]{2,1,0:T(8,128)(2,1)} %gather_fusion.5, pred[4]{0:T(512)(128)(4,1)S(1)} %copy-done.11), kind=kOutput, calls=%fused_computation.15 | convolution fusion | flops 2721447936 | bytes 16515080 | tf_op jit(solution)/shard_map/psx,psy->sxy/dot_general | solution.py:46
  170.1 12.5 %reshape.90 = f32[4,2,384,2,384]{4,3,2,1,0:T(2,128)} reshape(f32[4,768,768]{2,1,0:T(8,128)} %fusion.7) | data formatting | bytes 18874368 | tf_op jit(solution)/shard_map/reshape | solution.py:11
  182.6 14.8 %copy.43 = f32[4,2,384,2,384]{2,4,3,1,0:T(8,128)} copy(f32[4,2,384,2,384]{4,3,2,1,0:T(2,128)} %reshape.90) | data formatting | bytes 18874368 | tf_op jit(solution)/shard_map/reshape | solution.py:11
  199.9 0.7 gather_fusion.2
  200.7 0.7 broadcast_subtract_fusion
  201.4 164.2 %all-reduce.4.cloned.1.call-done = f32[4,2,384,2,384]{2,4,3,1,0:T(8,128)} async-done(((f32[4,2,384,2,384]{2,4,3,1,0:T(8,128)}), f32[4,2,384,2,384]{2,4,3,1,0:T(8,128)}) %all-reduce.4.cloned.1.call-update) | async-done | bytes 9437200 | tf_op jit(solution)/shard_map/psum | solution.py:50
  365.6 9.6 %copy.44 = f32[4,2,384,2,384]{4,2,3,1,0:T(8,128)} copy(f32[4,2,384,2,384]{2,4,3,1,0:T(8,128)} %all-reduce.4.cloned.1.call-done) | data formatting | bytes 18874368 | tf_op jit(solution)/shard_map/psum | solution.py:50
  375.2 9.6 %fusion.1 = bf16[4,2,384,2,384]{4,2,3,1,0:T(8,128)(2,1)} fusion(f32[4,2,384,2,384]{2,4,3,1,0:T(8,128)} %all-reduce.4.cloned.1.call-done, f32[4,2,384,2,384]{4,2,3,1,0:T(8,128)} %copy.44, f32[384]{0:T(512)S(1)} %copy-done.3, f32[4,2,384,2]{2,3,1,0:T(2,128)} %broadcast_subtract_fusion), kind=kLoop, calls=%fused_computation.9 | loop fusion | flops 11796480 | bytes 23619072 | tf_op jit(solution)/shard_map/convert_element_type | solution.py:20
  384.8 6.7 copy.52
  391.5 9.3 %copy.45 = bf16[4,2,384,2,384]{4,3,2,1,0:T(2,128)(2,1)} copy(bf16[4,2,384,2,384]{4,2,3,1,0:T(8,128)(2,1)} %fusion.1) | data formatting | bytes 9437184 | tf_op jit(solution)/shard_map/convert_element_type | solution.py:20
  400.8 11.3 %reshape.92 = bf16[4,768,768]{2,1,0:T(8,128)(2,1)} reshape(bf16[4,2,384,2,384]{4,3,2,1,0:T(2,128)(2,1)} %copy.45) | data formatting | bytes 9437184 | tf_op jit(solution)/shard_map/reshape | solution.py:20
  412.1 9.4 %fusion.15 = f32[576,4,768]{2,0,1:T(8,128)} fusion(bf16[4,768,768]{2,1,0:T(8,128)(2,1)} %reshape.92, bf16[4,576,768]{2,1,0:T(8,128)(2,1)} %gather_fusion.5, pred[4]{0:T(512)(128)(4,1)S(1)} %copy-done.12), kind=kOutput, calls=%fused_computation.23 | convolution fusion | flops 2719678464 | bytes 15335428 | tf_op jit(solution)/shard_map/sxy,psx->psy/dot_general | solution.py:53
  421.5 5.2 fusion.12
  426.8 3.3 convolution_bitcast_fusion
  430.1 17.5 %fusion.3 = f32[576,768,8]{1,2,0:T(8,128)} fusion(f32[576,4,768]{2,0,1:T(8,128)} %fusion.12, s32[4]{0:T(128)S(1)} %copy-done.5), kind=kOutput, calls=%fused_computation.11 | convolution fusion | flops 169869344 | bytes 21233680 | tf_op jit(solution)/shard_map/sk,psx->pkx/dot_general | solution.py:63
  447.6 16.5 %all-reduce.6.cloned.1.call-done = f32[384,384]{1,0:T(8,128)} async-done(((f32[384,384]{1,0:T(8,128)}), f32[384,384]{1,0:T(8,128)}) %all-reduce.6.cloned.1.call-update) | async-done | bytes 589840 | tf_op jit(solution)/shard_map/psum | solution.py:68
  464.2 20.2 %add_bitcast_fusion = f32[576,8,768]{2,1,0:T(8,128)} fusion(f32[576,768,8]{1,2,0:T(8,128)} %fusion.3, f32[576,4,768]{2,0,1:T(8,128)} %fusion.15, s32[4]{0:T(128)S(1)} %copy-done.7), kind=kOutput, calls=%fused_computation.6 | convolution fusion | flops 173408288 | bytes 35389456 | tf_op jit(solution)/shard_map/sk,psx->pkx/dot_general | solution.py:65
  484.4 14.7 %copy.48 = f32[576,8,768]{2,0,1:T(8,128)} copy(f32[576,8,768]{2,1,0:T(8,128)} %add_bitcast_fusion) | data formatting | bytes 28311552 | tf_op jit(solution)/shard_map/add | solution.py:63
  499.1 41.5 %all-reduce.8.cloned.1.call-done = f32[384,384]{1,0:T(8,128)} async-done(((f32[384,384]{1,0:T(8,128)}), f32[384,384]{1,0:T(8,128)}) %all-reduce.8.cloned.1.call-update) | async-done | bytes 589840 | tf_op jit(solution)/shard_map/psum | solution.py:68
  540.6 1.9 broadcast_multiply_fusion
  542.5 229.9 %reduce-scatter.2.cloned.1.call-done = f32[576,1,768]{2,0,1:T(8,128)} async-done(((f32[576,8,768]{2,0,1:T(8,128)}), f32[576,1,768]{2,0,1:T(8,128)}) %reduce-scatter.2.cloned.1.call-update) | async-done | bytes 1769488 | tf_op jit(solution)/shard_map/reduce_scatter | solution.py:66
  772.5 3.1 reshape.93
  (51 shorter events, 4.0 us)
Async XLA Ops:
  7.2 4.3 copy-start
  7.2 115.4 %all-gather.2.cloned.1.call-start = ((), (), s32[]{:S(2)}) async-start(), calls=%async_computation.1 | async-start | bytes 7962624 | tf_op jit(solution)/shard_map/all_gather | solution.py:34
  11.4 354.2 %all-reduce.4.cloned.1.call-start = ((), (), s32[]{:S(2)}) async-start(), calls=%async_computation.2 | async-start | bytes 18874368 | tf_op jit(solution)/shard_map/psum | solution.py:50
  12.1 120.6 %copy-start.4 = (s32[4]{0:T(128)}, s32[4]{0:T(128)S(1)}, u32[]{:S(2)}) copy-start(s32[4]{0:T(128)S(1)} %gather_fusion.1) | copy-start | bytes 52
  13.4 184.7 %copy-start.6 = (s32[4]{0:T(128)}, s32[4]{0:T(128)S(1)}, u32[]{:S(2)}) copy-start(s32[4]{0:T(128)S(1)} %gather_fusion) | copy-start | bytes 52
  14.0 146.8 %copy-start.9 = (pred[4]{0:T(512)(128)(4,1)}, pred[4]{0:T(512)(128)(4,1)S(1)}, u32[]{:S(2)}) copy-start(pred[4]{0:T(512)(128)(4,1)S(1)} %get-tuple-element.4) | copy-start | bytes 16
  157.0 3.8 copy-start.11
  197.4 0.7 copy-start.8
  197.4 3.3 copy-start.3
  197.4 266.7 %all-reduce.6.cloned.1.call-start = ((), (), s32[]{:S(2)}) async-start(), calls=%async_computation.4 | async-start | bytes 1179648 | tf_op jit(solution)/shard_map/psum | solution.py:68
  400.8 11.4 %copy-start.12 = (pred[4]{0:T(512)(128)(4,1)S(1)}, pred[4]{0:T(512)(128)(4,1)}, u32[]{:S(2)}) copy-start(pred[4]{0:T(512)(128)(4,1)} %get-tuple-element.3) | copy-start | bytes 16
  412.1 9.4 %copy-start.2 = (bf16[4,768,768]{2,1,0:T(8,128)(2,1)S(1)}, bf16[4,768,768]{2,1,0:T(8,128)(2,1)}, u32[]{:S(2)}) copy-start(bf16[4,768,768]{2,1,0:T(8,128)(2,1)} %reshape.92) | copy-start | bytes 14155780
  412.1 9.4 %copy-start.10 = (pred[4]{0:T(512)(128)(4,1)S(1)}, pred[4]{0:T(512)(128)(4,1)}, u32[]{:S(2)}) copy-start(pred[4]{0:T(512)(128)(4,1)} %copy-done.9) | copy-start | bytes 16
  421.5 8.6 %copy-start.5 = (s32[4]{0:T(128)S(1)}, s32[4]{0:T(128)}, u32[]{:S(2)}) copy-start(s32[4]{0:T(128)} %copy-done.4) | copy-start | bytes 52
  430.1 34.1 %copy-start.7 = (s32[4]{0:T(128)S(1)}, s32[4]{0:T(128)}, u32[]{:S(2)}) copy-start(s32[4]{0:T(128)} %copy-done.6) | copy-start | bytes 52
  430.1 110.6 %all-reduce.8.cloned.1.call-start = ((), (), s32[]{:S(2)}) async-start(), calls=%async_computation.5 | async-start | bytes 1179648 | tf_op jit(solution)/shard_map/psum | solution.py:68
  464.1 308.3 %reduce-scatter.2.cloned.1.call-start = ((), (), s32[]{:S(2)}) async-start(), calls=%async_computation.3 | async-start | bytes 15925248 | tf_op jit(solution)/shard_map/reduce_scatter | solution.py:66
  499.1 276.5 %copy-start.1 = (s32[32,1]{0,1:T(1,128)S(1)}, s32[32,1]{0,1:T(1,128)}, u32[]{:S(2)}) copy-start(s32[32,1]{0,1:T(1,128)} %param.12) | copy-start | bytes 388
Sparse Core Ops, SparseCore 0:
  11.5 111.0 all-gather.1
  197.6 167.9 all-reduce.3
  430.2 33.8 all-reduce.5
  467.3 73.2 all-reduce.7
  544.1 228.3 reduce-scatter.1
